TPU v7x, 32 devices: a whole 2x2x4 slice. The times are simulated.
32 devices in a mesh: groups: 2 (over y), tok: 4 (over z), slot: 2 (over x), hid: 2 (over core).
Axes of the slice: x: 2, y: 2, z: 4, core: 2. Of those that a mesh axis runs over, the one named last changes fastest.
Arguments:
- tokens: bfloat16 [8192, 1024], P(('groups', 'tok', 'slot', 'hid')), parts along dimension 0, may hold values from -12 to 12
- slot_keys: bfloat16 [2048, 512], P('groups', 'slot'), parts along dimension 0, may hold values from -12 to 12
- w_in: bfloat16 [4, 4, 1024, 4096], P(('groups', 'slot'), 'tok', None, 'hid'), parts along dimension 0, may hold values from -0.1875 to 0.1875
- w_out: bfloat16 [4, 4, 4096, 1024], P(('groups', 'slot'), 'tok', 'hid'), parts along dimension 0, may hold values from -0.09375 to 0.09375
Outputs:
- mixed: float32 [8192, 1024], P(('groups', 'tok', 'slot', 'hid')), parts along dimension 0
There are 2 independent parts, one for each index of `groups`. A program takes and returns all parts, laid end to end along the dimension named above; each array names one. Nothing has to cross between parts.
All inputs are finite; a program needn't handle non-finite values.
Results may differ from a plain program's by a relative error of at most 0.0022.
Values may be sent and summed in bfloat16 or wider, within the bound.
No kernel may reach another device: no remote copies, remote signals or barrier semaphores. Data moves between devices by JAX's collectives and lax.ppermute only.
A program may use at most 64 MiB of HBM per device.

v0:
```python
import jax
import jax.numpy as jnp
from jax import lax
from jax.sharding import PartitionSpec as P

epsilon = 1e-06


def local(tokens, slot_keys, w_in, w_out):
    model_width = tokens.shape[1]
    block_width = slot_keys.shape[1]
    owned_slots = block_width // (lax.axis_size("tok") * lax.axis_size("hid"))
    key_scale = lax.rsqrt(jnp.mean(jnp.square(slot_keys.astype(jnp.float32)), axis=0) + epsilon)
    fragment = lax.all_gather(tokens, "slot", axis=0, tiled=True)
    token_scale = lax.rsqrt(jnp.mean(jnp.square(fragment.astype(jnp.float32)), axis=1) + epsilon)
    logits = (
        4.0
        * token_scale[:, None]
        * key_scale[None, :]
        * jnp.dot(fragment, slot_keys, preferred_element_type=jnp.float32)
        / model_width
    )
    weights_exp = jnp.exp(logits)
    weights_low = weights_exp.astype(jnp.bfloat16)
    slot_numer = lax.dot_general(
        weights_low, fragment, (((0,), (0,)), ((), ())), preferred_element_type=jnp.float32
    )
    slot_denom = jnp.sum(weights_exp, axis=0)
    weights_all = weights_low
    token_denom = jnp.sum(weights_exp, axis=1)
    slot_numer, slot_denom, weights_all, token_denom = (
        slot_numer,
        slot_denom,
        weights_all,
        token_denom,
    )
    summed_numer, summed_denom = lax.psum((slot_numer, slot_denom), ("tok", "hid"))
    first_slot = lax.axis_index(("tok", "hid")) * owned_slots
    owned_numer = lax.dynamic_slice_in_dim(summed_numer, first_slot, owned_slots, 0)
    owned_denom = lax.dynamic_slice_in_dim(summed_denom, first_slot, owned_slots, 0)
    owned_inputs = (owned_numer / owned_denom[:, None]).astype(jnp.bfloat16)
    expert_inputs = lax.all_gather(owned_inputs, "hid", axis=0, tiled=True)
    hidden = jax.nn.gelu(
        jnp.dot(expert_inputs, w_in[0, 0], preferred_element_type=jnp.float32), approximate=True
    ).astype(jnp.bfloat16)
    half_outputs = jnp.dot(hidden, w_out[0, 0], preferred_element_type=jnp.float32)
    owned_outputs = lax.psum_scatter(half_outputs, "hid", scatter_dimension=0, tiled=True).astype(
        jnp.bfloat16
    )
    block_outputs = lax.all_gather(owned_outputs, ("tok", "hid"), axis=0, tiled=True)
    token_numer = jnp.dot(weights_all, block_outputs, preferred_element_type=jnp.float32)
    mine_numer, mine_denom = (
        lax.psum_scatter(token_numer, "slot", scatter_dimension=0, tiled=True),
        lax.psum_scatter(token_denom, "slot", scatter_dimension=0, tiled=True),
    )
    return mine_numer / mine_denom[:, None]


def solution(mesh):
    in_specs = (
        P(("groups", "tok", "slot", "hid"), None),
        P("groups", "slot"),
        P(("groups", "slot"), "tok", None, "hid"),
        P(("groups", "slot"), "tok", "hid", None),
    )
    out_specs = P(("groups", "tok", "slot", "hid"), None)
    return jax.shard_map(local, mesh=mesh, in_specs=in_specs, out_specs=out_specs, check_vma=False)
```

profile of v0, /device:TPU:0, one launch (start us, length us, event | category | flops | bytes accessed | tf_op | source)
XLA Modules:
  0.0 172.2 jit_solution(18349934714928174129)
XLA Ops:
  6.5 0.0 all-gather.2.cloned.1.call-start
  6.5 0.7 all-gather.2.cloned.1.call-update
  7.3 0.0 all-reduce.3.cloned.1.call-start
  7.3 1.2 multiply_reduce_fusion.1
  8.5 24.4 %all-gather.2.cloned.1.call-done = bf16[512,1024]{1,0:T(8,128)(2,1)} async-done(((bf16[256,1024]{1,0:T(8,128)(2,1)}), bf16[512,1024]{1,0:T(8,128)(2,1)}) %all-gather.2.cloned.1.call-update) | async-done | bytes 1048592 | tf_op jit(solution)/shard_map/all_gather | solution.py:14
  32.9 0.0 copy-start
  32.9 1.6 multiply_reduce_fusion
  34.5 1.9 %fusion.32 = (f32[512]{0:T(512)S(1)}, f32[256]{0:T(256)S(1)}, bf16[512,256]{1,0:T(8,128)(2,1)S(1)}) fusion(bf16[512,1024]{1,0:T(8,128)(2,1)} %all-gather.2.cloned.1.call-done, bf16[1024,256]{1,0:T(8,128)(2,1)} %param.5, f32[256]{0:T(256)S(1)} %add_rsqrt_fusion, f32[512]{0:T(512)S(1)} %rsqrt_multiply_fusion), kind=kOutput, calls=%fused_computation.34 | convolution fusion | flops 269221120 | bytes 1841152 | tf_op jit(solution)/shard_map/dot_general | solution.py:20
  36.4 0.0 copy-done
  36.4 1.4 fusion.26
  37.9 0.0 all-reduce.3.cloned.1.call-update
  37.9 0.0 reduce-scatter.3.cloned.1.call-start
  38.0 16.4 %psum.15 = f32[256]{0:T(256)S(1)} all-reduce(f32[256]{0:T(256)S(1)} %get-tuple-element.6), channel_id=1, replica_groups=mesh['groups'=2,'tok'=4,'slot'=2,'hid'=2] {'tok','hid'}, use_global_device_ids=true, to_apply=%region_4.0 | all-reduce | flops 256 | bytes 2048 | tf_op jit(solution)/shard_map/psum | solution.py:37
  54.4 0.1 dynamic_slice.7
  54.5 42.5 %all-reduce.3.cloned.1.call-done = f32[256,1024]{1,0:T(8,128)} async-done(((f32[256,1024]{1,0:T(8,128)}), f32[256,1024]{1,0:T(8,128)}) %all-reduce.3.cloned.1.call-update) | async-done | bytes 1048592 | tf_op jit(solution)/shard_map/psum | solution.py:37
  97.0 1.0 divide_convert_fusion
  98.0 1.9 %all_gather.10 = bf16[64,1024]{1,0:T(8,128)(2,1)S(1)} all-gather(bf16[32,1024]{1,0:T(8,128)(2,1)S(1)} %divide_convert_fusion), channel_id=1, replica_groups=mesh['groups'=2,'tok'=4,'slot'=2,'hid'=2] {'hid'}, dimensions={0}, use_global_device_ids=true | all-gather | bytes 196608 | tf_op jit(solution)/shard_map/all_gather | solution.py:42
  99.9 5.9 %fusion = f32[64,1024]{1,0:T(8,128)} fusion(bf16[1,1,2048,1024]{3,2,1,0:T(8,128)(2,1)} %param.7, bf16[64,1024]{1,0:T(8,128)(2,1)S(1)} %all_gather.10, bf16[1,1,1024,2048]{3,2,1,0:T(8,128)(2,1)} %param.6), kind=kOutput, calls=%fused_computation | convolution fusion | flops 538050560 | bytes 8781824 | tf_op jit(solution)/shard_map/dot_general | solution.py:46
  105.7 0.0 copy-start.1
  105.7 0.0 reduce-scatter.3.cloned.1.call-update
  105.7 0.0 reduce-scatter.5.cloned.1.call-start
  105.8 6.7 %reduce-scatter.3.cloned.1.call-done = f32[32,1024]{1,0:T(8,128)} async-done(((f32[64,1024]{1,0:T(8,128)}), f32[32,1024]{1,0:T(8,128)}) %reduce-scatter.3.cloned.1.call-update) | async-done | bytes 131088 | tf_op jit(solution)/shard_map/reduce_scatter | solution.py:47
  112.5 0.9 convert_element_type.23
  113.4 15.0 %all_gather.11 = bf16[256,1024]{1,0:T(8,128)(2,1)S(1)} all-gather(bf16[32,1024]{1,0:T(8,128)(2,1)S(1)} %convert_element_type.23), channel_id=1, replica_groups=mesh['groups'=2,'tok'=4,'slot'=2,'hid'=2] {'tok','hid'}, dimensions={0}, use_global_device_ids=true | all-gather | bytes 589824 | tf_op jit(solution)/shard_map/all_gather | solution.py:50
  128.4 1.8 %fusion.24 = f32[512,1024]{1,0:T(8,128)} fusion(bf16[256,1024]{1,0:T(8,128)(2,1)S(1)} %all_gather.11, bf16[512,256]{1,0:T(8,128)(2,1)S(1)} %get-tuple-element.7), kind=kOutput, calls=%fused_computation.24 | convolution fusion | flops 268435456 | bytes 2883584 | tf_op jit(solution)/shard_map/dot_general | solution.py:51
  130.2 0.0 reduce-scatter.5.cloned.1.call-update
  130.2 0.0 copy-done.1
  130.3 0.6 dynamic-slice
  131.5 4.9 %all-reduce = f32[512]{0:T(512)S(1)} all-reduce(f32[512]{0:T(512)S(1)} %get-tuple-element.5), channel_id=4, replica_groups=mesh['groups'=2,'tok'=4,'slot'=2,'hid'=2] {'slot'}, use_global_device_ids=true, to_apply=%region_8.0.clone | all-reduce | flops 512 | bytes 4096
  136.4 0.1 dynamic-slice.1
  136.5 26.8 %reduce-scatter.5.cloned.1.call-done = f32[256,1024]{1,0:T(8,128)} async-done(((f32[512,1024]{1,0:T(8,128)}), f32[256,1024]{1,0:T(8,128)}) %reduce-scatter.5.cloned.1.call-update) | async-done | bytes 1048592 | tf_op jit(solution)/shard_map/reduce_scatter | solution.py:53
  163.3 2.3 %broadcast_divide_fusion = f32[256,1024]{1,0:T(8,128)} fusion(f32[256,1024]{1,0:T(8,128)} %reduce-scatter.5.cloned.1.call-done, f32[256]{0:T(256)S(1)} %dynamic-slice.1), kind=kLoop, calls=%fused_computation.18 | loop fusion | flops 262144 | bytes 2098176 | tf_op jit(solution)/shard_map/div | solution.py:56
  (2 shorter events, 0.0 us)
Async XLA Ops:
  6.5 26.4 %all-gather.2.cloned.1.call-start = ((), (), s32[]{:S(2)}) async-start(), calls=%async_computation.2 | async-start | bytes 1572864 | tf_op jit(solution)/shard_map/all_gather | solution.py:14
  7.3 89.7 %all-reduce.3.cloned.1.call-start = ((), (), s32[]{:S(2)}) async-start(), calls=%async_computation.3 | async-start | bytes 2097152 | tf_op jit(solution)/shard_map/psum | solution.py:37
  32.9 3.5 %copy-start = (bf16[512,1024]{1,0:T(8,128)(2,1)S(1)}, bf16[512,1024]{1,0:T(8,128)(2,1)}, u32[]{:S(2)}) copy-start(bf16[512,1024]{1,0:T(8,128)(2,1)} %all-gather.2.cloned.1.call-done) | copy-start | bytes 3145732
  37.9 74.6 %reduce-scatter.3.cloned.1.call-start = ((), (), s32[]{:S(2)}) async-start(), calls=%async_computation.4 | async-start | bytes 393216 | tf_op jit(solution)/shard_map/reduce_scatter | solution.py:47
  105.7 24.5 %copy-start.1 = (u32[32]{0:T(128)S(1)}, u32[32]{0:T(128)}, u32[]{:S(2)}) copy-start(u32[32]{0:T(128)} %constant.43) | copy-start | bytes 388
  105.7 57.6 %reduce-scatter.5.cloned.1.call-start = ((), (), s32[]{:S(2)}) async-start(), calls=%async_computation.5 | async-start | bytes 3145728 | tf_op jit(solution)/shard_map/reduce_scatter | solution.py:53
Sparse Core Ops, SparseCore 0:
  8.9 23.9 all-gather.1
  38.0 58.8 all-reduce.2
  105.9 6.6 reduce-scatter.2
  130.4 32.8 reduce-scatter.4
where the time goes:
time: 173 us; the launch traced here: 172 us
  waiting for transfers between devices  101 us (58%)
  blocking collectives  38.2 us (22%)
  between operations  13.8 us (8%)
  matrix products  11 us (6%)
  other arithmetic  7.06 us (4%)
    psum x1, waiting for transfers between devices, local(): lax.psum((slot_numer, slot_denom), ('tok', 'hid'))  42.5 us
    reduce_scatter x1, waiting for transfers between devices, local(): lax.psum_scatter(token_numer, 'slot', scatter_dimension=0, tiled=True)  26.8 us
    all_gather x1, waiting for transfers between devices, local(): fragment = lax.all_gather(tokens, 'slot', axis=0, tiled=True)  24.4 us
    psum x1, blocking collectives, local(): lax.psum((slot_numer, slot_denom), ('tok', 'hid'))  16.4 us
    all_gather x1, blocking collectives, local(): lax.all_gather(owned_outputs, ('tok', 'hid'), axis=0, tiled=True)  15 us
    reduce_scatter x1, waiting for transfers between devices, local(): lax.psum_scatter(half_outputs, 'hid', scatter_dimension=0, tiled=True)  6.72 us
    dot_general x1, matrix products, local(): jnp.dot(hidden, w_out[0, 0], preferred_element_type=jnp.float32)  5.86 us
    unnamed x1, blocking collectives  4.94 us
  transfers between devices with their start and end apart: 4, of which 4 were waited for; matrix products, arithmetic and copies ran while one was open for 1% of the time, Pallas kernels for 0%

commit v1 on v0

--- a/solution.py
+++ b/solution.py
@@ -4,6 +4,12 @@
 from jax.sharding import PartitionSpec as P
 
 epsilon = 1e-06
+
+
+def in_order(parts, dim):
+    dims = list(parts.shape[1:])
+    dims[dim] *= parts.shape[0]
+    return jnp.moveaxis(parts, 0, dim).reshape(dims)
 
 
 def local(tokens, slot_keys, w_in, w_out):
@@ -47,7 +53,19 @@
     owned_outputs = lax.psum_scatter(half_outputs, "hid", scatter_dimension=0, tiled=True).astype(
         jnp.bfloat16
     )
-    block_outputs = lax.all_gather(owned_outputs, ("tok", "hid"), axis=0, tiled=True)
+    size = lax.axis_size(("tok", "hid"))
+    pairs = [(i, (i + 1) % size) for i in range(size)]
+    back = [(b, a) for a, b in pairs]
+    lower, upper = ([], [])
+    for hop in range(size - 1):
+        if hop % 2 == 0:
+            lower.append(lax.ppermute(lower[-1] if lower else owned_outputs, ("tok", "hid"), pairs))
+        else:
+            upper.append(lax.ppermute(upper[-1] if upper else owned_outputs, ("tok", "hid"), back))
+    blocks = jnp.stack([*lower[::-1], owned_outputs, *upper])
+    shift = lax.axis_index(("tok", "hid")) - len(lower)
+    blocks = blocks[(jnp.arange(size) - shift) % size]
+    block_outputs = in_order(blocks, 0)
     token_numer = jnp.dot(weights_all, block_outputs, preferred_element_type=jnp.float32)
     mine_numer, mine_denom = (
         lax.psum_scatter(token_numer, "slot", scatter_dimension=0, tiled=True),

time: 173 us -> 181 us (1.046)
  blocking collectives: 38.2 us -> 23.3 us
  waiting for transfers between devices: 101 us -> 112 us
  starting transfers between devices: 0.12 us -> 11.1 us
    all_gather x1 -> x0, blocking collectives: 15 us -> none  [local(): lax.all_gather(owned_outputs, ('tok', 'hid'), axis=0, tiled=True)]
    ppermute x0 -> x7, waiting for transfers between devices: none -> 11.5 us  [the longest x4 11.5 us: local(): lax.ppermute(lower[-1] if lower else owned_outputs, ('tok', 'hid'), pairs)]
    ppermute x0 -> x7, starting transfers between devices: none -> 11 us  [the longest x3 10.7 us: local(): lax.ppermute(upper[-1] if upper else owned_outputs, ('tok', 'hid'), back)]
  transfers between devices with their start and end apart: 4 -> 11, of which waited for: 4 -> 8; matrix products, arithmetic and copies ran while one was open for 1% -> 2% of each run, Pallas kernels for 0% -> 0%
where the time goes in v1:
time: 181 us
  waiting for transfers between devices  112 us (62%)
  blocking collectives  23.3 us (13%)
  between operations  13.9 us (8%)
  starting transfers between devices  11.1 us (6%)
  matrix products  11 us (6%)
  other arithmetic  8 us (4%)
    psum x1, waiting for transfers between devices, local(): lax.psum((slot_numer, slot_denom), ('tok', 'hid'))  42.5 us
    reduce_scatter x1, waiting for transfers between devices, local(): lax.psum_scatter(token_numer, 'slot', scatter_dimension=0, tiled=True)  26.5 us
    all_gather x1, waiting for transfers between devices, local(): fragment = lax.all_gather(tokens, 'slot', axis=0, tiled=True)  24.4 us
    psum x1, blocking collectives, local(): lax.psum((slot_numer, slot_denom), ('tok', 'hid'))  16.4 us
    ppermute x4, waiting for transfers between devices, local(): lax.ppermute(lower[-1] if lower else owned_outputs, ('tok', 'hid'), pairs)  11.5 us
    ppermute x3, starting transfers between devices, local(): lax.ppermute(upper[-1] if upper else owned_outputs, ('tok', 'hid'), back)  10.7 us
    reduce_scatter x1, waiting for transfers between devices, local(): lax.psum_scatter(half_outputs, 'hid', scatter_dimension=0, tiled=True)  6.72 us
    dot_general x1, matrix products, local(): jnp.dot(hidden, w_out[0, 0], preferred_element_type=jnp.float32)  5.86 us
  transfers between devices with their start and end apart: 11, of which 8 were waited for; matrix products, arithmetic and copies ran while one was open for 2% of the time, Pallas kernels for 0%

profile of v1, /device:TPU:0, one launch (start us, length us, event | category | flops | bytes accessed | tf_op | source)
XLA Modules:
  0.0 180.9 jit_solution(279190170544671520)
XLA Ops:
  6.5 0.7 all-gather.2.cloned.1.call-update
  7.3 1.2 multiply_reduce_fusion.1
  8.5 24.4 %all-gather.2.cloned.1.call-done = bf16[512,1024]{1,0:T(8,128)(2,1)} async-done(((bf16[256,1024]{1,0:T(8,128)(2,1)}), bf16[512,1024]{1,0:T(8,128)(2,1)}) %all-gather.2.cloned.1.call-update) | async-done | bytes 1048592 | tf_op jit(solution)/shard_map/all_gather | solution.py:20
  32.9 1.6 multiply_reduce_fusion
  34.5 1.9 %fusion.34 = (f32[512]{0:T(512)S(1)}, f32[256]{0:T(256)S(1)}, bf16[512,256]{1,0:T(8,128)(2,1)S(1)}) fusion(bf16[512,1024]{1,0:T(8,128)(2,1)} %all-gather.2.cloned.1.call-done, bf16[1024,256]{1,0:T(8,128)(2,1)} %param.5, f32[256]{0:T(256)S(1)} %add_rsqrt_fusion, f32[512]{0:T(512)S(1)} %rsqrt_multiply_fusion), kind=kOutput, calls=%fused_computation.50 | convolution fusion | flops 269221120 | bytes 1841152 | tf_op jit(solution)/shard_map/dot_general | solution.py:26
  36.4 1.4 fusion.26
  37.9 0.0 reduce-scatter.3.cloned.1.call-start
  38.0 16.4 %psum.15 = f32[256]{0:T(256)S(1)} all-reduce(f32[256]{0:T(256)S(1)} %get-tuple-element.6), channel_id=1, replica_groups=mesh['groups'=2,'tok'=4,'slot'=2,'hid'=2] {'tok','hid'}, use_global_device_ids=true, to_apply=%region_4.0 | all-reduce | flops 256 | bytes 2048 | tf_op jit(solution)/shard_map/psum | solution.py:43
  54.4 0.1 dynamic_slice.7
  54.5 42.5 %all-reduce.3.cloned.1.call-done = f32[256,1024]{1,0:T(8,128)} async-done(((f32[256,1024]{1,0:T(8,128)}), f32[256,1024]{1,0:T(8,128)}) %all-reduce.3.cloned.1.call-update) | async-done | bytes 1048592 | tf_op jit(solution)/shard_map/psum | solution.py:43
  97.0 1.0 divide_convert_fusion
  98.0 1.9 %all_gather.7 = bf16[64,1024]{1,0:T(8,128)(2,1)S(1)} all-gather(bf16[32,1024]{1,0:T(8,128)(2,1)S(1)} %divide_convert_fusion), channel_id=1, replica_groups=mesh['groups'=2,'tok'=4,'slot'=2,'hid'=2] {'hid'}, dimensions={0}, use_global_device_ids=true | all-gather | bytes 196608 | tf_op jit(solution)/shard_map/all_gather | solution.py:48
  99.9 5.9 %fusion = f32[64,1024]{1,0:T(8,128)} fusion(bf16[1,1,2048,1024]{3,2,1,0:T(8,128)(2,1)} %param.7, bf16[64,1024]{1,0:T(8,128)(2,1)S(1)} %all_gather.7, bf16[1,1,1024,2048]{3,2,1,0:T(8,128)(2,1)} %param.6), kind=kOutput, calls=%fused_computation.1 | convolution fusion | flops 538050560 | bytes 8781824 | tf_op jit(solution)/shard_map/dot_general | solution.py:52
  105.7 0.0 reduce-scatter.5.cloned.1.call-start
  105.8 6.7 %reduce-scatter.3.cloned.1.call-done = f32[32,1024]{1,0:T(8,128)} async-done(((f32[64,1024]{1,0:T(8,128)}), f32[32,1024]{1,0:T(8,128)}) %reduce-scatter.3.cloned.1.call-update) | async-done | bytes 131088 | tf_op jit(solution)/shard_map/reduce_scatter | solution.py:53
  112.5 0.9 convert_element_type.23
  113.4 0.2 collective-permute-start
  113.7 5.3 %collective-permute-done = bf16[32,1024]{1,0:T(8,128)(2,1)S(1)} collective-permute-done((bf16[32,1024]{1,0:T(8,128)(2,1)S(1)}, bf16[32,1024]{1,0:T(8,128)(2,1)S(1)}, u32[]{:S(2)}, u32[]{:S(2)}) %collective-permute-start) | collective-permute-done | bytes 65568 | tf_op jit(solution)/shard_map/ppermute | solution.py:62
  119.0 3.5 %collective-permute-start.4 = (bf16[32,1024]{1,0:T(8,128)(2,1)S(1)}, bf16[32,1024]{1,0:T(8,128)(2,1)S(1)}, u32[]{:S(2)}, u32[]{:S(2)}) collective-permute-start(bf16[32,1024]{1,0:T(8,128)(2,1)S(1)} %convert_element_type.23), channel_id=1, source_target_pairs={{1,0},{4,1},{5,4},{8,5},{9,8},{12,9},{13,12},{0,13},{3,2},{6,3},{7... | collective-permute-start | bytes 196616 | tf_op jit(solution)/shard_map/ppermute | solution.py:64
  122.5 2.4 %collective-permute-done.1 = bf16[32,1024]{1,0:T(8,128)(2,1)S(1)} collective-permute-done((bf16[32,1024]{1,0:T(8,128)(2,1)S(1)}, bf16[32,1024]{1,0:T(8,128)(2,1)S(1)}, u32[]{:S(2)}, u32[]{:S(2)}) %collective-permute-start.1) | collective-permute-done | bytes 65568 | tf_op jit(solution)/shard_map/ppermute | solution.py:62
  124.9 3.6 %collective-permute-start.5 = (bf16[32,1024]{1,0:T(8,128)(2,1)S(1)}, bf16[32,1024]{1,0:T(8,128)(2,1)S(1)}, u32[]{:S(2)}, u32[]{:S(2)}) collective-permute-start(bf16[32,1024]{1,0:T(8,128)(2,1)S(1)} %collective-permute-done.4), channel_id=1, source_target_pairs={{1,0},{4,1},{5,4},{8,5},{9,8},{12,9},{13,12},{0,13},{3,2},{6,3},{7... | collective-permute-start | bytes 196616 | tf_op jit(solution)/shard_map/ppermute | solution.py:64
  128.5 1.9 %collective-permute-done.2 = bf16[32,1024]{1,0:T(8,128)(2,1)S(1)} collective-permute-done((bf16[32,1024]{1,0:T(8,128)(2,1)S(1)}, bf16[32,1024]{1,0:T(8,128)(2,1)S(1)}, u32[]{:S(2)}, u32[]{:S(2)}) %collective-permute-start.2) | collective-permute-done | bytes 65568 | tf_op jit(solution)/shard_map/ppermute | solution.py:62
  130.4 3.6 %collective-permute-start.6 = (bf16[32,1024]{1,0:T(8,128)(2,1)S(1)}, bf16[32,1024]{1,0:T(8,128)(2,1)S(1)}, u32[]{:S(2)}, u32[]{:S(2)}) collective-permute-start(bf16[32,1024]{1,0:T(8,128)(2,1)S(1)} %collective-permute-done.5), channel_id=1, source_target_pairs={{1,0},{4,1},{5,4},{8,5},{9,8},{12,9},{13,12},{0,13},{3,2},{6,3},{7... | collective-permute-start | bytes 196616 | tf_op jit(solution)/shard_map/ppermute | solution.py:64
  134.0 1.9 %collective-permute-done.3 = bf16[32,1024]{1,0:T(8,128)(2,1)S(1)} collective-permute-done((bf16[32,1024]{1,0:T(8,128)(2,1)S(1)}, bf16[32,1024]{1,0:T(8,128)(2,1)S(1)}, u32[]{:S(2)}, u32[]{:S(2)}) %collective-permute-start.3) | collective-permute-done | bytes 65568 | tf_op jit(solution)/shard_map/ppermute | solution.py:62
  136.0 0.9 bitcast_dynamic-update-slice_fusion.3
  136.9 0.6 gather_fusion
  137.5 1.8 fusion.24
  139.3 0.6 dynamic-slice
  140.6 4.9 %all-reduce = f32[512]{0:T(512)S(1)} all-reduce(f32[512]{0:T(512)S(1)} %get-tuple-element.5), channel_id=4, replica_groups=mesh['groups'=2,'tok'=4,'slot'=2,'hid'=2] {'slot'}, use_global_device_ids=true, to_apply=%region_8.9.clone | all-reduce | flops 512 | bytes 4096
  145.5 0.1 dynamic-slice.1
  145.6 26.5 %reduce-scatter.5.cloned.1.call-done = f32[256,1024]{1,0:T(8,128)} async-done(((f32[512,1024]{1,0:T(8,128)}), f32[256,1024]{1,0:T(8,128)}) %reduce-scatter.5.cloned.1.call-update) | async-done | bytes 1048592 | tf_op jit(solution)/shard_map/reduce_scatter | solution.py:71
  172.0 2.3 %broadcast_divide_fusion = f32[256,1024]{1,0:T(8,128)} fusion(f32[256,1024]{1,0:T(8,128)} %reduce-scatter.5.cloned.1.call-done, f32[256]{0:T(256)S(1)} %dynamic-slice.1), kind=kLoop, calls=%fused_computation.19 | loop fusion | flops 262144 | bytes 2098176 | tf_op jit(solution)/shard_map/div | solution.py:74
  (26 shorter events, 0.2 us)
Async XLA Ops:
  6.5 26.4 %all-gather.2.cloned.1.call-start = ((), (), s32[]{:S(2)}) async-start(), calls=%async_computation.2 | async-start | bytes 1572864 | tf_op jit(solution)/shard_map/all_gather | solution.py:20
  7.3 89.7 %all-reduce.3.cloned.1.call-start = ((), (), s32[]{:S(2)}) async-start(), calls=%async_computation.3 | async-start | bytes 2097152 | tf_op jit(solution)/shard_map/psum | solution.py:43
  32.9 3.5 %copy-start = (bf16[512,1024]{1,0:T(8,128)(2,1)S(1)}, bf16[512,1024]{1,0:T(8,128)(2,1)}, u32[]{:S(2)}) copy-start(bf16[512,1024]{1,0:T(8,128)(2,1)} %all-gather.2.cloned.1.call-done) | copy-start | bytes 3145732
  37.9 74.6 %reduce-scatter.3.cloned.1.call-start = ((), (), s32[]{:S(2)}) async-start(), calls=%async_computation.4 | async-start | bytes 393216 | tf_op jit(solution)/shard_map/reduce_scatter | solution.py:53
  105.7 33.6 %copy-start.1 = (u32[32]{0:T(128)S(1)}, u32[32]{0:T(128)}, u32[]{:S(2)}) copy-start(u32[32]{0:T(128)} %constant.62) | copy-start | bytes 388
  105.7 66.3 %reduce-scatter.5.cloned.1.call-start = ((), (), s32[]{:S(2)}) async-start(), calls=%async_computation.5 | async-start | bytes 3145728 | tf_op jit(solution)/shard_map/reduce_scatter | solution.py:71
  113.4 5.5 %collective-permute-start = (bf16[32,1024]{1,0:T(8,128)(2,1)S(1)}, bf16[32,1024]{1,0:T(8,128)(2,1)S(1)}, u32[]{:S(2)}, u32[]{:S(2)}) collective-permute-start(bf16[32,1024]{1,0:T(8,128)(2,1)S(1)} %convert_element_type.23), channel_id=1, source_target_pairs={{0,1},{1,4},{4,5},{5,8},{8,9},{9,12},{12,13},{13,0},{2,3},{3,6},{6... | collective-permute-start | bytes 196616 | tf_op jit(solution)/shard_map/ppermute | solution.py:62
  119.0 5.9 %collective-permute-start.1 = (bf16[32,1024]{1,0:T(8,128)(2,1)S(1)}, bf16[32,1024]{1,0:T(8,128)(2,1)S(1)}, u32[]{:S(2)}, u32[]{:S(2)}) collective-permute-start(bf16[32,1024]{1,0:T(8,128)(2,1)S(1)} %collective-permute-done), channel_id=1, source_target_pairs={{0,1},{1,4},{4,5},{5,8},{8,9},{9,12},{12,13},{13,0},{2,3},{3,6},{6... | collective-permute-start | bytes 196616 | tf_op jit(solution)/shard_map/ppermute | solution.py:62
  119.0 5.9 %collective-permute-start.4 = (bf16[32,1024]{1,0:T(8,128)(2,1)S(1)}, bf16[32,1024]{1,0:T(8,128)(2,1)S(1)}, u32[]{:S(2)}, u32[]{:S(2)}) collective-permute-start(bf16[32,1024]{1,0:T(8,128)(2,1)S(1)} %convert_element_type.23), channel_id=1, source_target_pairs={{1,0},{4,1},{5,4},{8,5},{9,8},{12,9},{13,12},{0,13},{3,2},{6,3},{7... | collective-permute-start | bytes 196616 | tf_op jit(solution)/shard_map/ppermute | solution.py:64
  124.9 5.5 %collective-permute-start.2 = (bf16[32,1024]{1,0:T(8,128)(2,1)S(1)}, bf16[32,1024]{1,0:T(8,128)(2,1)S(1)}, u32[]{:S(2)}, u32[]{:S(2)}) collective-permute-start(bf16[32,1024]{1,0:T(8,128)(2,1)S(1)} %collective-permute-done.1), channel_id=1, source_target_pairs={{0,1},{1,4},{4,5},{5,8},{8,9},{9,12},{12,13},{13,0},{2,3},{3,6},{6... | collective-permute-start | bytes 196616 | tf_op jit(solution)/shard_map/ppermute | solution.py:62
  124.9 5.5 %collective-permute-start.5 = (bf16[32,1024]{1,0:T(8,128)(2,1)S(1)}, bf16[32,1024]{1,0:T(8,128)(2,1)S(1)}, u32[]{:S(2)}, u32[]{:S(2)}) collective-permute-start(bf16[32,1024]{1,0:T(8,128)(2,1)S(1)} %collective-permute-done.4), channel_id=1, source_target_pairs={{1,0},{4,1},{5,4},{8,5},{9,8},{12,9},{13,12},{0,13},{3,2},{6,3},{7... | collective-permute-start | bytes 196616 | tf_op jit(solution)/shard_map/ppermute | solution.py:64
  130.4 5.5 %collective-permute-start.3 = (bf16[32,1024]{1,0:T(8,128)(2,1)S(1)}, bf16[32,1024]{1,0:T(8,128)(2,1)S(1)}, u32[]{:S(2)}, u32[]{:S(2)}) collective-permute-start(bf16[32,1024]{1,0:T(8,128)(2,1)S(1)} %collective-permute-done.2), channel_id=1, source_target_pairs={{0,1},{1,4},{4,5},{5,8},{8,9},{9,12},{12,13},{13,0},{2,3},{3,6},{6... | collective-permute-start | bytes 196616 | tf_op jit(solution)/shard_map/ppermute | solution.py:62
  130.4 6.5 %collective-permute-start.6 = (bf16[32,1024]{1,0:T(8,128)(2,1)S(1)}, bf16[32,1024]{1,0:T(8,128)(2,1)S(1)}, u32[]{:S(2)}, u32[]{:S(2)}) collective-permute-start(bf16[32,1024]{1,0:T(8,128)(2,1)S(1)} %collective-permute-done.5), channel_id=1, source_target_pairs={{1,0},{4,1},{5,4},{8,5},{9,8},{12,9},{13,12},{0,13},{3,2},{6,3},{7... | collective-permute-start | bytes 196616 | tf_op jit(solution)/shard_map/ppermute | solution.py:64
Sparse Core Ops, SparseCore 0:
  8.9 23.9 all-gather.1
  38.0 58.8 all-reduce.2
  105.9 6.6 reduce-scatter.2
  139.4 32.5 reduce-scatter.4
